TPU v7x, 32 devices: a whole 2x2x4 slice. The times are simulated.
32 devices in a mesh: groups: 2 (over y), dp: 16 (over z, x, core).
Axes of the slice: x: 2, y: 2, z: 4, core: 2. Of those that a mesh axis runs over, the one named last changes fastest.
Arguments:
- queries: bfloat16 [16384, 4096], P(('groups', 'dp')), parts along dimension 0, may hold values from -100 to 100
- resp_kv: bfloat16 [16384, 2, 512], P(('groups', 'dp')), parts along dimension 0, may hold values from -6 to 6
- prompt_kv: bfloat16 [8192, 2, 512], P(('groups', 'dp')), parts along dimension 0, may hold values from -6 to 6
- groups: int32 [64], P(('groups', 'dp')), parts along dimension 0, may hold values from 0 to 15, as said below
- resp_lengths: int32 [64], P(('groups', 'dp')), parts along dimension 0, may hold values from 64 to 256, as said below
- prompt_lengths: int32 [32], P('groups'), parts along dimension 0, may hold values from 64 to 256, as said below
Outputs:
- attended: bfloat16 [16384, 4096], P(('groups', 'dp')), parts along dimension 0
There are 2 independent parts, one for each index of `groups`. A program takes and returns all parts, laid end to end along the dimension named above; each array names one. Nothing has to cross between parts.
Inputs may be any that keep to these rules, and one draw needn't show every extreme that they name: `groups`: entry n is the prompt whose rows response n reads; some prompts are read by many responses. `resp_lengths`: rows at and after the length are padding. `prompt_lengths`: key rows at and after the length are padding.
All inputs are finite; a program needn't handle non-finite values.
Results may differ from a plain program's by a relative error of at most 0.0043.
Values may be sent and summed in bfloat16 or wider, within the bound.
No kernel may reach another device: no remote copies, remote signals or barrier semaphores. Data moves between devices by JAX's collectives and lax.ppermute only.
A program may use at most 128 MiB of HBM per device.

v0:
```python
import functools
import math

import jax
import jax.numpy as jnp
from jax import lax
from jax.experimental import pallas as pl
from jax.experimental.pallas import tpu as pltpu
from jax.sharding import PartitionSpec as P


KV_HEADS = 4
HEAD_DIM = 128
TILE = 16

masked_score = -1e30
FOLD = math.log2(math.e) / math.sqrt(HEAD_DIM)
MOST_TOTAL = 2.0**60
PIECE = 2
OWN_PIECE = 4


def split_pairs(pairs):
    count = pairs.shape[0]
    half = count // 2
    row = lax.broadcasted_iota(jnp.int32, (count, count), 0)
    col = lax.broadcasted_iota(jnp.int32, (count, count), 1)
    source = jnp.where(row < half, 2 * row, 2 * (row - half) + 1)
    chosen = jnp.where(col == source, 1.0, 0.0).astype(pairs.dtype)
    return jnp.dot(chosen, pairs, preferred_element_type=jnp.float32).astype(pairs.dtype)


def select_kernel(half, place_ref, in_ref, after_ref, second_ref, *refs):
    by_distance, (vec_ref, idx_ref, sem, sems) = refs[:half], refs[half:]
    rows = second_ref.shape[1]
    wanted = in_ref[:, rows:, :].astype(jnp.float32)
    vec_ref[...] = wanted[:, 0, :].astype(jnp.int32)
    copy = pltpu.make_async_copy(vec_ref, idx_ref, sem)
    copy.start()
    copy.wait()
    place = place_ref[0]
    start = place_ref[1]
    copies = []
    for k in range(half):
        for slot, target, out in (
            (1, k, second_ref.at[k]),
            (0, jnp.bitwise_xor(place, k), by_distance[k]),
        ):
            copies.append(
                pltpu.make_async_copy(
                    in_ref.at[idx_ref[start + target, slot], pl.ds(0, rows)], out, sems.at[slot, k]
                )
            )
            copies[-1].start()
    for copy in copies:
        copy.wait()


def scores_of(queries, keys):
    return lax.dot_general(
        queries, keys, (((1,), (1,)), ((), ())), preferred_element_type=jnp.float32
    )


def with_ones(values):
    return jnp.concatenate([values, jnp.ones(values.shape, values.dtype)], axis=1)


def stacked(ref, rows, heads):
    return jnp.concatenate(
        [ref[rows, head * HEAD_DIM : (head + 1) * HEAD_DIM] for head in heads], axis=0
    )


def own_kernel(per_group, q_ref, kv_ref, *refs):
    out_ref, sum_ref = refs[-2:]
    size = q_ref.shape[0]
    half = size // 2
    split = split_pairs(kv_ref[...].reshape(2 * size, HEAD_DIM))
    keys = split[:size]
    values = with_ones(split[size:])
    causal = lax.broadcasted_iota(jnp.int32, (half, half), 1) <= lax.broadcasted_iota(
        jnp.int32, (half, half), 0
    )
    causal = jnp.concatenate([causal.astype(jnp.float32)] * OWN_PIECE, axis=0) > 0.5
    lane = lax.broadcasted_iota(jnp.int32, (half, HEAD_DIM), 1)
    totals = [jnp.ones((half, HEAD_DIM), jnp.float32)] * 2
    pieces = [
        (part, range(first, first + OWN_PIECE))
        for first in range(0, per_group, OWN_PIECE)
        for part in range(2)
    ]
    score, weight = {}, {}
    for step in range(len(pieces) + 2):
        if step < len(pieces):
            part, heads = pieces[step]
            rows = slice(part * half, (part + 1) * half)
            score[step] = scores_of(stacked(q_ref, rows, heads), keys[: (part + 1) * half])
        if step >= 2:
            part, heads = pieces[step - 2]
            sums = jnp.dot(
                weight.pop(step - 2), values[: (part + 1) * half], preferred_element_type=jnp.float32
            )
            for place, head in enumerate(heads):
                rows = slice(place * half, (place + 1) * half)
                out_ref[part * half : (part + 1) * half, head * HEAD_DIM : (head + 1) * HEAD_DIM] = (
                    sums[rows, :HEAD_DIM].astype(out_ref.dtype)
                )
                totals[part] = jnp.where(lane == head, sums[rows, HEAD_DIM:], totals[part])
        if 1 <= step <= len(pieces):
            part, heads = pieces[step - 1]
            raw = score.pop(step - 1)
            last = jnp.where(causal, jnp.exp2(raw[:, part * half :] * FOLD), 0.0).astype(jnp.bfloat16)
            if part:
                before = jnp.exp2(raw[:, :half] * FOLD).astype(jnp.bfloat16)
                last = jnp.concatenate([before, last], axis=1)
            weight[step - 1] = last
    for part in range(2):
        sum_ref[part * half : (part + 1) * half, :] = totals[part]


def prompt_kernel(per_group, slot, count, *refs):
    place_ref, groups_ref, lives_ref, plens_ref, q_ref, kv_ref, own_ref, sum_ref = refs[:8]
    blocks, (out_ref, pairs_ref, sem) = refs[8 : 8 + 2 * count], refs[-3:]
    size = q_ref.shape[0]
    live = plens_ref[groups_ref[slot]]
    rows_live = lives_ref[slot]
    keys, values = (
        jnp.concatenate([ref[...].reshape(-1, HEAD_DIM) for ref in part], axis=0)
        for part in (blocks[:count], blocks[count:])
    )
    position = lax.broadcasted_iota(jnp.int32, (keys.shape[0], HEAD_DIM), 0)
    if count > 1:
        sliver = keys.shape[0] // count
        position = jnp.bitwise_xor(position, place_ref[0] * sliver)
    keys = jnp.where(position < live, keys.astype(jnp.float32), 0.0).astype(keys.dtype)
    alive = jnp.where(position < live, 1.0, 0.0)
    values = jnp.concatenate(
        [values.astype(jnp.float32) * alive, alive], axis=1
    ).astype(values.dtype)
    kept = lax.broadcasted_iota(jnp.int32, (size, HEAD_DIM), 0) < rows_live
    pieces = [range(first, first + PIECE) for first in range(0, per_group, PIECE)]
    score, weight = {}, {}
    most = jnp.zeros((8, HEAD_DIM), jnp.float32)
    least = jnp.min(sum_ref[...].reshape(-1, 8, HEAD_DIM), axis=0)
    for step in range(len(pieces) + 2):
        if step < len(pieces):
            score[step] = scores_of(stacked(q_ref, slice(None), pieces[step]), keys)
        if step >= 2:
            sums = jnp.dot(weight.pop(step - 2), values, preferred_element_type=jnp.float32)
            for place, head in enumerate(pieces[step - 2]):
                rows = slice(place * size, (place + 1) * size)
                cols = slice(head * HEAD_DIM, (head + 1) * HEAD_DIM)
                total = sums[rows, HEAD_DIM:] + sum_ref[:, head : head + 1]
                most = jnp.maximum(most, jnp.max(total.reshape(-1, 8, HEAD_DIM), axis=0))
                result = (sums[rows, :HEAD_DIM] + own_ref[:, cols].astype(jnp.float32)) / total
                out_ref[:, cols] = jnp.where(kept, result, 0.0).astype(out_ref.dtype)
        if 1 <= step <= len(pieces):
            weight[step - 1] = jnp.exp2(score.pop(step - 1) * FOLD).astype(jnp.bfloat16)
    sound = jnp.logical_and(least > 1.0 / MOST_TOTAL, most < MOST_TOTAL)

    @pl.when(jnp.min(jnp.where(sound, 1.0, 0.0)) < 0.5)
    def _():
        first = pl.multiple_of(pl.program_id(0) * HEAD_DIM, HEAD_DIM)
        copy = pltpu.make_async_copy(
            kv_ref.at[pl.ds(slot * size, size), :, pl.ds(first, HEAD_DIM)], pairs_ref, sem
        )
        copy.start()
        copy.wait()
        split = split_pairs(pairs_ref[...].reshape(2 * size, HEAD_DIM))
        own_keys = split[:size]
        own_values = with_ones(split[size:])
        row = lax.broadcasted_iota(jnp.int32, (size, size), 0)
        key = lax.broadcasted_iota(jnp.int32, (size, size), 1)

        def exact(head, carry):
            cols = pl.ds(pl.multiple_of(head * HEAD_DIM, HEAD_DIM), HEAD_DIM)
            queries = q_ref[:, cols]
            prompt = scores_of(queries, keys)
            key_place = lax.broadcasted_iota(jnp.int32, prompt.shape, 1)
            if count > 1:
                key_place = jnp.bitwise_xor(key_place, place_ref[0] * sliver)
            prompt = jnp.where(key_place < live, prompt, masked_score)
            own = jnp.where(key <= row, scores_of(queries, own_keys), masked_score)
            top = FOLD * jnp.maximum(
                jnp.max(prompt, axis=1, keepdims=True), jnp.max(own, axis=1, keepdims=True)
            )
            sums = jnp.dot(
                jnp.exp2(prompt * FOLD - top).astype(jnp.bfloat16),
                values,
                preferred_element_type=jnp.float32,
            )
            sums += jnp.dot(
                jnp.exp2(own * FOLD - top).astype(jnp.bfloat16),
                own_values,
                preferred_element_type=jnp.float32,
            )
            result = sums[:, :HEAD_DIM] / sums[:, HEAD_DIM:]
            out_ref[:, cols] = jnp.where(kept, result, 0.0).astype(out_ref.dtype)
            return carry

        lax.fori_loop(0, per_group, exact, 0)


def params(mib=60):
    return pltpu.CompilerParams(vmem_limit_bytes=mib * 1024 * 1024)


def fetch_fast(prompt_kv, groups, devices, after):
    slots = groups.shape[0]
    prompt_len = prompt_kv.shape[0]
    half = devices // 2
    rows = 2 * KV_HEADS * (prompt_len // half)
    smem = pl.BlockSpec(memory_space=pltpu.SMEM)
    vmem = pl.BlockSpec(memory_space=pltpu.VMEM)
    anywhere = pl.BlockSpec(memory_space=pl.ANY)
    slivers = prompt_kv.reshape(half, prompt_len // half, 2, KV_HEADS, HEAD_DIM)
    slivers = jnp.transpose(slivers, (0, 2, 3, 1, 4)).reshape(half, rows, HEAD_DIM)
    wanted = jnp.pad(groups.astype(jnp.bfloat16), (0, HEAD_DIM - slots))
    wanted = jnp.broadcast_to(wanted, (devices, 8, HEAD_DIM))
    packed = jnp.concatenate([jnp.concatenate([slivers, slivers], axis=0), wanted], axis=1)
    spread = lax.all_to_all(packed, "dp", split_axis=0, concat_axis=0, tiled=True)
    index = lax.axis_index("dp")
    place = lax.rem(index, half)
    piece = jax.ShapeDtypeStruct((rows, HEAD_DIM), jnp.bfloat16)
    second, *rest = pl.pallas_call(
        functools.partial(select_kernel, half),
        out_shape=[jax.ShapeDtypeStruct((half, rows, HEAD_DIM), jnp.bfloat16)] + [piece] * half,
        in_specs=[smem, vmem, anywhere],
        out_specs=[anywhere] * (1 + half),
        scratch_shapes=[
            pltpu.VMEM((devices, HEAD_DIM), jnp.int32),
            pltpu.SMEM((devices, HEAD_DIM), jnp.int32),
            pltpu.SemaphoreType.DMA,
            pltpu.SemaphoreType.DMA((slots, half)),
        ],
        compiler_params=params(4),
        name="select",
    )(
        jnp.stack([place, index - place]),
        spread,
        pltpu.with_memory_space_constraint(after, pltpu.HBM),
    )
    halves = [list(range(half)), list(range(half, devices))]
    for k in range(1, half):
        rest[k] = lax.ppermute(rest[k], "dp", [(i, i ^ k) for i in range(devices)])
    second = lax.all_to_all(
        second, "dp", split_axis=0, concat_axis=0, tiled=True, axis_index_groups=halves
    )
    return [rest, [second]], place


def fetch_plain(prompt_kv, groups, devices):
    slots = groups.shape[0]
    prompt_len, _, width = prompt_kv.shape
    sliver = prompt_len // devices
    wanted = lax.all_gather(groups, "dp", axis=0, tiled=True)
    by_prompt = lax.all_to_all(
        prompt_kv.reshape(devices, sliver, 2, width), "dp", split_axis=0, concat_axis=0, tiled=True
    )
    chosen = jnp.take(by_prompt, wanted, axis=0).reshape(devices, slots, sliver, 2, width)
    fetched = lax.all_to_all(chosen, "dp", split_axis=0, concat_axis=0, tiled=True)
    whole = jnp.transpose(fetched, (1, 0, 2, 3, 4))
    whole = whole.reshape(slots, -1, TILE, 2, KV_HEADS, HEAD_DIM)
    whole = jnp.transpose(whole, (1, 0, 3, 4, 2, 5))
    whole = whole.reshape(whole.shape[0], slots, 2 * KV_HEADS * TILE, HEAD_DIM)
    return [[whole[:, slot]] for slot in range(slots)], jnp.int32(0)


def on_device(queries, resp_kv, prompt_kv, groups, resp_lengths, prompt_lengths):
    devices = lax.axis_size("dp")
    slots = groups.shape[0]
    resp_len = queries.shape[0] // slots
    width = queries.shape[1] // KV_HEADS
    per_group = width // HEAD_DIM
    prompt_len = prompt_kv.shape[0]
    heads = KV_HEADS * per_group
    scores = heads * resp_len * resp_len
    moved = queries.size

    own_shapes = (
        jax.ShapeDtypeStruct(queries.shape, jnp.bfloat16),
        jax.ShapeDtypeStruct((queries.shape[0], KV_HEADS * HEAD_DIM), jnp.float32),
    )
    own_steps = []
    for slot in range(slots):
        before = own_steps[-1] if own_steps else ()
        own_steps.append(
            pl.pallas_call(
                functools.partial(own_kernel, per_group),
                grid=(KV_HEADS,),
                out_shape=own_shapes,
                in_specs=[
                    pl.BlockSpec((resp_len, width), lambda c, slot=slot: (slot, c)),
                    pl.BlockSpec((resp_len, 2, HEAD_DIM), lambda c, slot=slot: (slot, 0, c)),
                ]
                + [pl.BlockSpec(memory_space=pl.ANY)] * len(before),
                out_specs=(
                    pl.BlockSpec((resp_len, width), lambda c, slot=slot: (slot, c)),
                    pl.BlockSpec((resp_len, HEAD_DIM), lambda c, slot=slot: (slot, c)),
                ),
                input_output_aliases={2 + i: i for i in range(len(before))},
                compiler_params=params(),
                cost_estimate=pl.CostEstimate(
                    flops=scores * HEAD_DIM * 4,
                    bytes_accessed=moved * 6 // slots,
                    transcendentals=scores,
                ),
            )(queries, resp_kv, *before)
        )
    own = [pltpu.with_memory_space_constraint(part, pltpu.HBM) for part in own_steps[-1]]
    queries = pltpu.with_memory_space_constraint(queries, pltpu.HBM)
    resp_kv = pltpu.with_memory_space_constraint(resp_kv, pltpu.HBM)

    half = devices // 2
    if slots == 2 and devices & (devices - 1) == 0 and prompt_len % (half * TILE) == 0:
        fetched, place = fetch_fast(prompt_kv, groups, devices, own[1])
    else:
        fetched, place = fetch_plain(prompt_kv, groups, devices)
    place = place.reshape(1)

    out = None
    for slot in range(slots):
        blocks = fetched[slot]
        q_spec = pl.BlockSpec((resp_len, width), lambda c, *_, slot=slot: (slot, c))

        def tile_spec(block, offset):
            rows = block.shape[-2] // (2 * KV_HEADS)
            lead = block.shape[:-2]
            return pl.BlockSpec(
                lead + (rows, HEAD_DIM), lambda c, *_: (0,) * len(lead) + (c + offset, 0)
            )

        out = pl.pallas_call(
            functools.partial(prompt_kernel, per_group, slot, len(blocks)),
            grid_spec=pltpu.PrefetchScalarGridSpec(
                num_scalar_prefetch=4,
                grid=(KV_HEADS,),
                in_specs=[
                    q_spec,
                    pl.BlockSpec(memory_space=pl.ANY),
                    q_spec,
                    pl.BlockSpec((resp_len, HEAD_DIM), lambda c, *_, slot=slot: (slot, c)),
                ]
                + [tile_spec(block, 0) for block in blocks]
                + [tile_spec(block, KV_HEADS) for block in blocks]
                + ([] if out is None else [pl.BlockSpec(memory_space=pl.ANY)]),
                out_specs=q_spec,
                scratch_shapes=[
                    pltpu.VMEM((resp_len, 2, HEAD_DIM), jnp.bfloat16),
                    pltpu.SemaphoreType.DMA,
                ],
            ),
            out_shape=jax.ShapeDtypeStruct(queries.shape, jnp.bfloat16),
            input_output_aliases={} if out is None else {8 + 2 * len(blocks): 0},
            compiler_params=params(32),
            cost_estimate=pl.CostEstimate(
                flops=scores * HEAD_DIM * 4,
                bytes_accessed=moved * 8 // slots,
                transcendentals=scores,
            ),
        )(
            place,
            groups,
            resp_lengths,
            prompt_lengths,
            queries,
            resp_kv,
            *own,
            *blocks,
            *blocks,
            *([] if out is None else [out]),
        )
    return out


def solution(mesh):
    return jax.shard_map(
        on_device,
        mesh=mesh,
        in_specs=(
            P(("groups", "dp"), None),
            P(("groups", "dp"), None, None),
            P(("groups", "dp"), None, None),
            P(("groups", "dp")),
            P(("groups", "dp")),
            P("groups"),
        ),
        out_specs=P(("groups", "dp"), None),
        check_vma=False,
    )
```

profile of v0, /device:TPU:0, one launch (start us, length us, event | category | flops | bytes accessed | tf_op | source)
XLA Modules:
  0.0 117.4 jit_solution(6913978732010954219)
XLA Ops:
  0.0 0.7 convert_element_type.5
  0.7 1.4 %reshape.10 = bf16[8,32,2,4,128]{4,3,2,1,0:T(4,128)(2,1)S(1)} reshape(bf16[256,2,512]{2,1,0:T(2,128)(2,1)} %param.8) | data formatting | bytes 1048576 | tf_op jit(solution)/shard_map/reshape | solution.py:217
  2.0 0.1 copy.10
  2.2 1.1 pad_maximum_fusion
  3.3 7.4 %all-to-all-start = ((bf16[16,264,128]{2,1,0:T(8,128)(2,1)}), bf16[16,264,128]{2,1,0:T(8,128)(2,1)S(1)}, u32[]{:S(2)}, u32[]{:S(2)}) async-start(bf16[16,264,128]{2,1,0:T(8,128)(2,1)} %pad_maximum_fusion), calls=%async_computation | async-start | bytes 2162688 | tf_op jit(solution)/shard_map/all_to_all | solution.py:222
  10.7 6.1 %shard_map.64 = (bf16[512,4096]{1,0:T(8,128)(2,1)}, f32[512,512]{1,0:T(8,128)}) custom-call(bf16[512,4096]{1,0:T(8,128)(2,1)} %refs_4_.3, bf16[512,2,512]{2,1,0:T(2,128)(2,1)} %refs_5_.3), custom_call_target="tpu_custom_call" | custom-call | flops 1073741824 | bytes 6291456 | tf_op jit(solution)/shard_map/pallas_call | solution.py:289
  16.8 6.2 %shard_map.65 = (bf16[512,4096]{1,0:T(8,128)(2,1)}, f32[512,512]{1,0:T(8,128)}) custom-call(bf16[512,4096]{1,0:T(8,128)(2,1)} %refs_4_.3, bf16[512,2,512]{2,1,0:T(2,128)(2,1)} %refs_5_.3, bf16[512,4096]{1,0:T(8,128)(2,1)} %get-tuple-element.18.refs_0_, f32[512,512]{1,0:T(8,128)} %get-tuple-element.19.refs_1_), custom_call_target="tpu_custom_call", output_to_operand_aliasing={{0}: (2, {}), {1}: (3, {})} | custom-call | flops 1073741824 | bytes 6291456 | tf_op jit(solution)/shard_map/pallas_call | solution.py:289
  23.0 0.0 copy-start
  23.0 0.0 copy-start.1
  23.0 0.0 copy-start.2
  23.0 0.1 pad_add_fusion.place_ref
  23.1 11.0 %all-to-all-done.in_ref = bf16[16,264,128]{2,1,0:T(8,128)(2,1)S(1)} async-done(((bf16[16,264,128]{2,1,0:T(8,128)(2,1)}), bf16[16,264,128]{2,1,0:T(8,128)(2,1)S(1)}, u32[]{:S(2)}, u32[]{:S(2)}) %all-to-all-start) | async-done | bytes 1081376 | tf_op jit(solution)/shard_map/all_to_all | solution.py:222
  34.1 2.6 %select.4 = (bf16[8,256,128]{2,1,0:T(8,128)(2,1)}, bf16[256,128]{1,0:T(8,128)(2,1)S(1)}, bf16[256,128]{1,0:T(8,128)(2,1)S(1)}, bf16[256,128]{1,0:T(8,128)(2,1)S(...) custom-call(s32[2]{0:T(128)S(1)} %pad_add_fusion.place_ref, ...), custom_call_target="tpu_custom_call" | custom-call | tf_op jit(solution)/shard_map/select/pallas_call | solution.py:226
  36.8 6.0 %all-to-all-start.1 = ((bf16[8,256,128]{2,1,0:T(8,128)(2,1)}), bf16[8,256,128]{2,1,0:T(8,128)(2,1)S(1)}, u32[]{:S(2)}, u32[]{:S(2)}) async-start(bf16[8,256,128]{2,1,0:T(8,128)(2,1)} %get-tuple-element.22), calls=%async_computation.1 | async-start | bytes 1048576 | tf_op jit(solution)/shard_map/all_to_all | solution.py:247
  42.7 0.5 collective-permute-start
  43.2 1.6 %collective-permute-start.1 = (bf16[256,128]{1,0:T(8,128)(2,1)S(1)}, bf16[256,128]{1,0:T(8,128)(2,1)S(1)}, u32[]{:S(2)}, u32[]{:S(2)}) collective-permute-start(bf16[256,128]{1,0:T(8,128)(2,1)S(1)} %get-tuple-element.25), channel_id=1, source_target_pairs={{0,2},{1,3},{2,0},{3,1},{4,6},{5,7},{6,4},{7,5},{8,10},{9,11},{10,... | collective-permute-start | bytes 196616 | tf_op jit(solution)/shard_map/ppermute | solution.py:246
  44.9 0.0 collective-permute-start.2
  44.9 1.7 %collective-permute-start.3 = (bf16[256,128]{1,0:T(8,128)(2,1)S(1)}, bf16[256,128]{1,0:T(8,128)(2,1)S(1)}, u32[]{:S(2)}, u32[]{:S(2)}) collective-permute-start(bf16[256,128]{1,0:T(8,128)(2,1)S(1)} %get-tuple-element.27), channel_id=1, source_target_pairs={{0,4},{1,5},{2,6},{3,7},{4,0},{5,1},{6,2},{7,3},{8,12},{9,13},{10,... | collective-permute-start | bytes 196616 | tf_op jit(solution)/shard_map/ppermute | solution.py:246
  46.6 0.1 collective-permute-start.4
  46.7 0.0 collective-permute-done.refs_9_.refs_17_
  46.7 2.5 %collective-permute-start.5 = (bf16[256,128]{1,0:T(8,128)(2,1)S(1)}, bf16[256,128]{1,0:T(8,128)(2,1)S(1)}, u32[]{:S(2)}, u32[]{:S(2)}) collective-permute-start(bf16[256,128]{1,0:T(8,128)(2,1)S(1)} %get-tuple-element.29), channel_id=1, source_target_pairs={{0,6},{1,7},{2,4},{3,5},{4,2},{5,3},{6,0},{7,1},{8,14},{9,15},{10,... | collective-permute-start | bytes 196616 | tf_op jit(solution)/shard_map/ppermute | solution.py:246
  49.3 4.2 %collective-permute-done.1.refs_10_.refs_18_ = bf16[256,128]{1,0:T(8,128)(2,1)S(1)} collective-permute-done((bf16[256,128]{1,0:T(8,128)(2,1)S(1)}, bf16[256,128]{1,0:T(8,128)(2,1)S(1)}, u32[]{:S(2)}, u32[]{:S(2)}) %collective-permute-start.1) | collective-permute-done | bytes 65568 | tf_op jit(solution)/shard_map/ppermute | solution.py:246
  53.5 0.3 collective-permute-start.6
  53.8 0.0 collective-permute-done.2.refs_11_.refs_19_
  53.8 0.0 collective-permute-done.3.refs_12_.refs_20_
  53.8 0.0 collective-permute-done.4.refs_13_.refs_21_
  53.8 2.9 %collective-permute-done.5.refs_14_.refs_22_ = bf16[256,128]{1,0:T(8,128)(2,1)S(1)} collective-permute-done((bf16[256,128]{1,0:T(8,128)(2,1)S(1)}, bf16[256,128]{1,0:T(8,128)(2,1)S(1)}, u32[]{:S(2)}, u32[]{:S(2)}) %collective-permute-start.5) | collective-permute-done | bytes 65568 | tf_op jit(solution)/shard_map/ppermute | solution.py:246
  56.7 1.4 %collective-permute-done.6.refs_15_.refs_23_ = bf16[256,128]{1,0:T(8,128)(2,1)S(1)} collective-permute-done((bf16[256,128]{1,0:T(8,128)(2,1)S(1)}, bf16[256,128]{1,0:T(8,128)(2,1)S(1)}, u32[]{:S(2)}, u32[]{:S(2)}) %collective-permute-start.6) | collective-permute-done | bytes 65568 | tf_op jit(solution)/shard_map/ppermute | solution.py:246
  58.1 0.0 copy-done
  58.1 0.0 copy-done.1
  58.1 0.0 copy-done.2
  58.1 29.7 %shard_map.66.refs_10_ = bf16[512,4096]{1,0:T(8,128)(2,1)} custom-call(s32[1]{0:T(128)} %bitcast.refs_0_, s32[2]{0:T(128)S(1)} %copy-done, s32[2]{0:T(128)S(1)} %copy-done.1, s32[16]{0:T(128)S(1)} %copy-done.2, bf16[512,4096]{1,0:T(8,128)(2,1)} %refs_4_.3, bf16[512,2,512]{2,1,0:T(2,128)(2,1)} %refs_5_.3, bf16[512,4096]{1,0:T(8,128)(2,1)} %get-tuple-element.20.refs_6_, ...), custom_call_target="tpu_custom_call" | custom-call | flops 1073741824 | bytes 8388608 | tf_op jit(solution)/shard_map/pallas_call | solution.py:334
  87.8 0.0 all-to-all-done.1.refs_8_.refs_9_
  87.8 29.6 %shard_map.67 = bf16[512,4096]{1,0:T(8,128)(2,1)} custom-call(s32[1]{0:T(128)} %bitcast.refs_0_, s32[2]{0:T(128)S(1)} %copy-done, s32[2]{0:T(128)S(1)} %copy-done.1, s32[16]{0:T(128)S(1)} %copy-done.2, bf16[512,4096]{1,0:T(8,128)(2,1)} %refs_4_.3, bf16[512,2,512]{2,1,0:T(2,128)(2,1)} %refs_5_.3, ...), custom_call_target="tpu_custom_call", output_to_operand_aliasing={{}: (10, {})} | custom-call | flops 1073741824 | bytes 8388608 | tf_op jit(solution)/shard_map/pallas_call | solution.py:334
  (2 shorter events, 0.0 us)
Async XLA Ops:
  3.3 30.8 %all-to-all-start = ((bf16[16,264,128]{2,1,0:T(8,128)(2,1)}), bf16[16,264,128]{2,1,0:T(8,128)(2,1)S(1)}, u32[]{:S(2)}, u32[]{:S(2)}) async-start(bf16[16,264,128]{2,1,0:T(8,128)(2,1)} %pad_maximum_fusion), calls=%async_computation | async-start | bytes 2162688 | tf_op jit(solution)/shard_map/all_to_all | solution.py:222
  23.0 35.1 %copy-start = (s32[2]{0:T(128)S(1)}, s32[2]{0:T(128)}, u32[]{:S(2)}) copy-start(s32[2]{0:T(128)} %refs_1_.3) | copy-start | bytes 28
  23.0 35.1 %copy-start.1 = (s32[2]{0:T(128)S(1)}, s32[2]{0:T(128)}, u32[]{:S(2)}) copy-start(s32[2]{0:T(128)} %refs_2_.3) | copy-start | bytes 28
  23.0 35.1 %copy-start.2 = (s32[16]{0:T(128)S(1)}, s32[16]{0:T(128)}, u32[]{:S(2)}) copy-start(s32[16]{0:T(128)} %refs_3_.3) | copy-start | bytes 196
  36.8 51.0 %all-to-all-start.1 = ((bf16[8,256,128]{2,1,0:T(8,128)(2,1)}), bf16[8,256,128]{2,1,0:T(8,128)(2,1)S(1)}, u32[]{:S(2)}, u32[]{:S(2)}) async-start(bf16[8,256,128]{2,1,0:T(8,128)(2,1)} %get-tuple-element.22), calls=%async_computation.1 | async-start | bytes 1048576 | tf_op jit(solution)/shard_map/all_to_all | solution.py:247
  42.7 4.0 %collective-permute-start = (bf16[256,128]{1,0:T(8,128)(2,1)S(1)}, bf16[256,128]{1,0:T(8,128)(2,1)S(1)}, u32[]{:S(2)}, u32[]{:S(2)}) collective-permute-start(bf16[256,128]{1,0:T(8,128)(2,1)S(1)} %get-tuple-element.24), channel_id=1, source_target_pairs={{0,1},{1,0},{2,3},{3,2},{4,5},{5,4},{6,7},{7,6},{8,9},{9,8},{10,11... | collective-permute-start | bytes 196616 | tf_op jit(solution)/shard_map/ppermute | solution.py:246
  43.2 10.3 %collective-permute-start.1 = (bf16[256,128]{1,0:T(8,128)(2,1)S(1)}, bf16[256,128]{1,0:T(8,128)(2,1)S(1)}, u32[]{:S(2)}, u32[]{:S(2)}) collective-permute-start(bf16[256,128]{1,0:T(8,128)(2,1)S(1)} %get-tuple-element.25), channel_id=1, source_target_pairs={{0,2},{1,3},{2,0},{3,1},{4,6},{5,7},{6,4},{7,5},{8,10},{9,11},{10,... | collective-permute-start | bytes 196616 | tf_op jit(solution)/shard_map/ppermute | solution.py:246
  44.9 9.0 %collective-permute-start.2 = (bf16[256,128]{1,0:T(8,128)(2,1)S(1)}, bf16[256,128]{1,0:T(8,128)(2,1)S(1)}, u32[]{:S(2)}, u32[]{:S(2)}) collective-permute-start(bf16[256,128]{1,0:T(8,128)(2,1)S(1)} %get-tuple-element.26), channel_id=1, source_target_pairs={{0,3},{1,2},{2,1},{3,0},{4,7},{5,6},{6,5},{7,4},{8,11},{9,10},{10,... | collective-permute-start | bytes 196616 | tf_op jit(solution)/shard_map/ppermute | solution.py:246
  44.9 9.0 %collective-permute-start.3 = (bf16[256,128]{1,0:T(8,128)(2,1)S(1)}, bf16[256,128]{1,0:T(8,128)(2,1)S(1)}, u32[]{:S(2)}, u32[]{:S(2)}) collective-permute-start(bf16[256,128]{1,0:T(8,128)(2,1)S(1)} %get-tuple-element.27), channel_id=1, source_target_pairs={{0,4},{1,5},{2,6},{3,7},{4,0},{5,1},{6,2},{7,3},{8,12},{9,13},{10,... | collective-permute-start | bytes 196616 | tf_op jit(solution)/shard_map/ppermute | solution.py:246
  46.6 7.2 %collective-permute-start.4 = (bf16[256,128]{1,0:T(8,128)(2,1)S(1)}, bf16[256,128]{1,0:T(8,128)(2,1)S(1)}, u32[]{:S(2)}, u32[]{:S(2)}) collective-permute-start(bf16[256,128]{1,0:T(8,128)(2,1)S(1)} %get-tuple-element.28), channel_id=1, source_target_pairs={{0,5},{1,4},{2,7},{3,6},{4,1},{5,0},{6,3},{7,2},{8,13},{9,12},{10,... | collective-permute-start | bytes 196616 | tf_op jit(solution)/shard_map/ppermute | solution.py:246
  46.7 10.0 %collective-permute-start.5 = (bf16[256,128]{1,0:T(8,128)(2,1)S(1)}, bf16[256,128]{1,0:T(8,128)(2,1)S(1)}, u32[]{:S(2)}, u32[]{:S(2)}) collective-permute-start(bf16[256,128]{1,0:T(8,128)(2,1)S(1)} %get-tuple-element.29), channel_id=1, source_target_pairs={{0,6},{1,7},{2,4},{3,5},{4,2},{5,3},{6,0},{7,1},{8,14},{9,15},{10,... | collective-permute-start | bytes 196616 | tf_op jit(solution)/shard_map/ppermute | solution.py:246
  53.5 4.6 %collective-permute-start.6 = (bf16[256,128]{1,0:T(8,128)(2,1)S(1)}, bf16[256,128]{1,0:T(8,128)(2,1)S(1)}, u32[]{:S(2)}, u32[]{:S(2)}) collective-permute-start(bf16[256,128]{1,0:T(8,128)(2,1)S(1)} %get-tuple-element.30), channel_id=1, source_target_pairs={{0,7},{1,6},{2,5},{3,4},{4,3},{5,2},{6,1},{7,0},{8,15},{9,14},{10,... | collective-permute-start | bytes 196616 | tf_op jit(solution)/shard_map/ppermute | solution.py:246
where the time goes:
time: 118 us; the launch traced here: 117 us
  Pallas kernels  74.2 us (63%)
  starting transfers between devices  20.2 us (17%)
  waiting for transfers between devices  19.6 us (17%)
  other arithmetic  1.86 us (2%)
  local copies, waits for them, and re-layouts  1.51 us (1%)
    pallas_call x2, Pallas kernels, on_device(): pl.pallas_call(functools.partial(prompt_kernel, per_group, slot, len(bloc...  59.3 us
    pallas_call x2, Pallas kernels, on_device(): pl.pallas_call(functools.partial(own_kernel, per_group), grid=(KV_HEADS,)...  12.3 us
    all_to_all x1, waiting for transfers between devices, fetch_fast(): lax.all_to_all(packed, 'dp', split_axis=0, concat_axis=0, tiled=True)  11 us
    ppermute x7, waiting for transfers between devices, fetch_fast(): rest[k] = lax.ppermute(rest[k], 'dp', [(i, i ^ k) for i in range(devices)])  8.52 us
    all_to_all x1, starting transfers between devices, fetch_fast(): lax.all_to_all(packed, 'dp', split_axis=0, concat_axis=0, tiled=True)  7.39 us
    ppermute x7, starting transfers between devices, fetch_fast(): rest[k] = lax.ppermute(rest[k], 'dp', [(i, i ^ k) for i in range(devices)])  6.85 us
    all_to_all x1, starting transfers between devices, fetch_fast(): lax.all_to_all(second, 'dp', split_axis=0, concat_axis=0, tiled=True, axi...  5.98 us
    pallas_call x1, Pallas kernels, fetch_fast(): pl.pallas_call(functools.partial(select_kernel, half), out_shape=[jax.Sha...  2.64 us
  transfers between devices with their start and end apart: 9, of which 4 were waited for; matrix products, arithmetic and copies ran while one was open for 0% of the time, Pallas kernels for 36%

commit v1 on v0

--- a/solution.py
+++ b/solution.py
@@ -30,26 +30,17 @@
     return jnp.dot(chosen, pairs, preferred_element_type=jnp.float32).astype(pairs.dtype)
 
 
-def select_kernel(half, place_ref, in_ref, after_ref, second_ref, *refs):
-    by_distance, (vec_ref, idx_ref, sem, sems) = refs[:half], refs[half:]
-    rows = second_ref.shape[1]
-    wanted = in_ref[:, rows:, :].astype(jnp.float32)
-    vec_ref[...] = wanted[:, 0, :].astype(jnp.int32)
-    copy = pltpu.make_async_copy(vec_ref, idx_ref, sem)
-    copy.start()
-    copy.wait()
-    place = place_ref[0]
-    start = place_ref[1]
+def select_kernel(half, place_ref, *refs):
+    asked, (in_ref, after_ref, second_ref) = refs[:half], refs[half : half + 3]
+    by_distance, sems = refs[half + 3 : -1], refs[-1]
     copies = []
     for k in range(half):
-        for slot, target, out in (
-            (1, k, second_ref.at[k]),
-            (0, jnp.bitwise_xor(place, k), by_distance[k]),
+        for slot, out in (
+            (1, second_ref.at[jnp.bitwise_xor(place_ref[0], k)]),
+            (0, by_distance[k]),
         ):
             copies.append(
-                pltpu.make_async_copy(
-                    in_ref.at[idx_ref[start + target, slot], pl.ds(0, rows)], out, sems.at[slot, k]
-                )
+                pltpu.make_async_copy(in_ref.at[asked[k][slot]], out, sems.at[slot, k])
             )
             copies[-1].start()
     for copy in copies:
@@ -216,28 +207,25 @@
     anywhere = pl.BlockSpec(memory_space=pl.ANY)
     slivers = prompt_kv.reshape(half, prompt_len // half, 2, KV_HEADS, HEAD_DIM)
     slivers = jnp.transpose(slivers, (0, 2, 3, 1, 4)).reshape(half, rows, HEAD_DIM)
-    wanted = jnp.pad(groups.astype(jnp.bfloat16), (0, HEAD_DIM - slots))
-    wanted = jnp.broadcast_to(wanted, (devices, 8, HEAD_DIM))
-    packed = jnp.concatenate([jnp.concatenate([slivers, slivers], axis=0), wanted], axis=1)
+    packed = jnp.concatenate([slivers, slivers], axis=0)
     spread = lax.all_to_all(packed, "dp", split_axis=0, concat_axis=0, tiled=True)
+    asked = [groups]
+    for k in range(1, half):
+        asked.append(lax.ppermute(groups, "dp", [(i, i ^ k) for i in range(devices)]))
     index = lax.axis_index("dp")
     place = lax.rem(index, half)
     piece = jax.ShapeDtypeStruct((rows, HEAD_DIM), jnp.bfloat16)
     second, *rest = pl.pallas_call(
         functools.partial(select_kernel, half),
         out_shape=[jax.ShapeDtypeStruct((half, rows, HEAD_DIM), jnp.bfloat16)] + [piece] * half,
-        in_specs=[smem, vmem, anywhere],
+        in_specs=[smem] * (1 + half) + [vmem, anywhere],
         out_specs=[anywhere] * (1 + half),
-        scratch_shapes=[
-            pltpu.VMEM((devices, HEAD_DIM), jnp.int32),
-            pltpu.SMEM((devices, HEAD_DIM), jnp.int32),
-            pltpu.SemaphoreType.DMA,
-            pltpu.SemaphoreType.DMA((slots, half)),
-        ],
+        scratch_shapes=[pltpu.SemaphoreType.DMA((slots, half))],
         compiler_params=params(4),
         name="select",
     )(
-        jnp.stack([place, index - place]),
+        place.reshape(1),
+        *asked,
         spread,
         pltpu.with_memory_space_constraint(after, pltpu.HBM),
     )

time: 118 us -> 116 us (0.983)
  waiting for transfers between devices: 19.6 us -> 11.7 us
  starting transfers between devices: 20.2 us -> 27.5 us
    all_to_all x1, waiting for transfers between devices: 11 us -> 0.91 us  [fetch_fast(): lax.all_to_all(packed, 'dp', split_axis=0, concat_axis=0, tiled=True)]
    ppermute x0 -> x7, starting transfers between devices: none -> 7.45 us  [fetch_fast(): lax.ppermute(groups, 'dp', [(i, i ^ k) for i in range(devices)])]
    ppermute x0 -> x7, waiting for transfers between devices: none -> 2.25 us  [fetch_fast(): lax.ppermute(groups, 'dp', [(i, i ^ k) for i in range(devices)])]
  transfers between devices with their start and end apart: 9 -> 16, of which waited for: 4 -> 5; matrix products, arithmetic and copies ran while one was open for 0% -> 0% of each run, Pallas kernels for 36% -> 36%
where the time goes in v1:
time: 116 us; the launch traced here: 115 us
  Pallas kernels  73.4 us (63%)
  starting transfers between devices  27.5 us (24%)
  waiting for transfers between devices  11.7 us (10%)
  local copies, waits for them, and re-layouts  1.51 us (1%)
    pallas_call x2, Pallas kernels, on_device(): pl.pallas_call(functools.partial(prompt_kernel, per_group, slot, len(bloc...  59.2 us
    pallas_call x2, Pallas kernels, on_device(): pl.pallas_call(functools.partial(own_kernel, per_group), grid=(KV_HEADS,)...  12.2 us
    ppermute x7, waiting for transfers between devices, fetch_fast(): rest[k] = lax.ppermute(rest[k], 'dp', [(i, i ^ k) for i in range(devices)])  8.52 us
    ppermute x7, starting transfers between devices, fetch_fast(): lax.ppermute(groups, 'dp', [(i, i ^ k) for i in range(devices)])  7.45 us
    all_to_all x1, starting transfers between devices, fetch_fast(): lax.all_to_all(packed, 'dp', split_axis=0, concat_axis=0, tiled=True)  7.39 us
    ppermute x7, starting transfers between devices, fetch_fast(): rest[k] = lax.ppermute(rest[k], 'dp', [(i, i ^ k) for i in range(devices)])  6.85 us
    all_to_all x1, starting transfers between devices, fetch_fast(): lax.all_to_all(second, 'dp', split_axis=0, concat_axis=0, tiled=True, axi...  5.8 us
  transfers between devices with their start and end apart: 16, of which 5 were waited for; matrix products, arithmetic and copies ran while one was open for 0% of the time, Pallas kernels for 36%

profile of v1, /device:TPU:0, one launch (start us, length us, event | category | flops | bytes accessed | tf_op | source)
XLA Modules:
  0.0 115.3 jit_solution(14439809583751178207)
XLA Ops:
  0.0 0.0 copy-start
  0.0 1.4 %reshape.11 = bf16[8,32,2,4,128]{4,3,2,1,0:T(4,128)(2,1)S(1)} reshape(bf16[256,2,512]{2,1,0:T(2,128)(2,1)} %param.8) | data formatting | bytes 1048576 | tf_op jit(solution)/shard_map/reshape | solution.py:208
  1.4 0.1 copy.10
  1.5 1.1 pad_maximum_fusion
  2.6 7.4 %all-to-all-start = ((bf16[16,256,128]{2,1,0:T(8,128)(2,1)}), bf16[16,256,128]{2,1,0:T(8,128)(2,1)S(1)}, u32[]{:S(2)}, u32[]{:S(2)}) async-start(bf16[16,256,128]{2,1,0:T(8,128)(2,1)} %pad_maximum_fusion), calls=%async_computation | async-start | bytes 2097152 | tf_op jit(solution)/shard_map/all_to_all | solution.py:211
  10.0 0.0 copy-done
  10.0 2.6 %collective-permute-start.6 = (s32[2]{0:T(128)S(1)}, s32[2]{0:T(128)S(1)}, u32[]{:S(2)}, u32[]{:S(2)}) collective-permute-start(s32[2]{0:T(128)S(1)} %copy-done), channel_id=1, source_target_pairs={{0,7},{1,6},{2,5},{3,4},{4,3},{5,2},{6,1},{7,0},{8,15},{9,14},{10,... | collective-permute-start | bytes 32 | tf_op jit(solution)/shard_map/ppermute | solution.py:214
  12.6 0.4 collective-permute-start.5
  13.0 1.4 %collective-permute-start.4 = (s32[2]{0:T(128)S(1)}, s32[2]{0:T(128)S(1)}, u32[]{:S(2)}, u32[]{:S(2)}) collective-permute-start(s32[2]{0:T(128)S(1)} %copy-done), channel_id=1, source_target_pairs={{0,5},{1,4},{2,7},{3,6},{4,1},{5,0},{6,3},{7,2},{8,13},{9,12},{10,... | collective-permute-start | bytes 32 | tf_op jit(solution)/shard_map/ppermute | solution.py:214
  14.3 0.3 collective-permute-start.3
  14.6 1.5 %collective-permute-start.2 = (s32[2]{0:T(128)S(1)}, s32[2]{0:T(128)S(1)}, u32[]{:S(2)}, u32[]{:S(2)}) collective-permute-start(s32[2]{0:T(128)S(1)} %copy-done), channel_id=1, source_target_pairs={{0,3},{1,2},{2,1},{3,0},{4,7},{5,6},{6,5},{7,4},{8,11},{9,10},{10,... | collective-permute-start | bytes 32 | tf_op jit(solution)/shard_map/ppermute | solution.py:214
  16.1 6.1 %shard_map.64 = (bf16[512,4096]{1,0:T(8,128)(2,1)}, f32[512,512]{1,0:T(8,128)}) custom-call(bf16[512,4096]{1,0:T(8,128)(2,1)} %refs_4_.3, bf16[512,2,512]{2,1,0:T(2,128)(2,1)} %refs_5_.3), custom_call_target="tpu_custom_call" | custom-call | flops 1073741824 | bytes 6291456 | tf_op jit(solution)/shard_map/pallas_call | solution.py:277
  22.2 0.0 copy-start.1
  22.2 0.0 copy-start.2
  22.2 6.1 %shard_map.65 = (bf16[512,4096]{1,0:T(8,128)(2,1)}, f32[512,512]{1,0:T(8,128)}) custom-call(bf16[512,4096]{1,0:T(8,128)(2,1)} %refs_4_.3, bf16[512,2,512]{2,1,0:T(2,128)(2,1)} %refs_5_.3, bf16[512,4096]{1,0:T(8,128)(2,1)} %get-tuple-element.18.refs_0_, f32[512,512]{1,0:T(8,128)} %get-tuple-element.19.refs_1_), custom_call_target="tpu_custom_call", output_to_operand_aliasing={{0}: (2, {}), {1}: (3, {})} | custom-call | flops 1073741824 | bytes 6291456 | tf_op jit(solution)/shard_map/pallas_call | solution.py:277
  28.3 0.0 collective-permute-done.6.refs_7_
  28.3 1.3 %collective-permute-start.1 = (s32[2]{0:T(128)S(1)}, s32[2]{0:T(128)S(1)}, u32[]{:S(2)}, u32[]{:S(2)}) collective-permute-start(s32[2]{0:T(128)S(1)} %copy-done), channel_id=1, source_target_pairs={{0,2},{1,3},{2,0},{3,1},{4,6},{5,7},{6,4},{7,5},{8,10},{9,11},{10,... | collective-permute-start | bytes 32 | tf_op jit(solution)/shard_map/ppermute | solution.py:214
  29.7 0.0 collective-permute-done.5.refs_6_
  29.7 0.0 collective-permute-start
  29.7 0.0 collective-permute-done.4.refs_5_
  29.7 0.0 collective-permute-done.3.refs_4_
  29.7 0.0 collective-permute-done.2.refs_3_
  29.7 2.2 %collective-permute-done.1.refs_2_ = s32[2]{0:T(128)S(1)} collective-permute-done((s32[2]{0:T(128)S(1)}, s32[2]{0:T(128)S(1)}, u32[]{:S(2)}, u32[]{:S(2)}) %collective-permute-start.1) | collective-permute-done | bytes 40 | tf_op jit(solution)/shard_map/ppermute | solution.py:214
  31.9 0.0 collective-permute-done.refs_1_
  31.9 0.9 all-to-all-done.refs_8_
  32.9 2.0 %select.3 = (bf16[8,256,128]{2,1,0:T(8,128)(2,1)}, bf16[256,128]{1,0:T(8,128)(2,1)S(1)}, bf16[256,128]{1,0:T(8,128)(2,1)S(1)}, bf16[256,128]{1,0:T(8,128)(2,1)S(...) custom-call(s32[1]{0:T(128)} %bitcast.place_ref.refs_0_, ...), custom_call_target="tpu_custom_call" | custom-call | tf_op jit(solution)/shard_map/select/pallas_call | solution.py:218
  34.9 5.8 %all-to-all-start.1 = ((bf16[8,256,128]{2,1,0:T(8,128)(2,1)}), bf16[8,256,128]{2,1,0:T(8,128)(2,1)S(1)}, u32[]{:S(2)}, u32[]{:S(2)}) async-start(bf16[8,256,128]{2,1,0:T(8,128)(2,1)} %get-tuple-element.22), calls=%async_computation.1 | async-start | bytes 1048576 | tf_op jit(solution)/shard_map/all_to_all | solution.py:235
  40.7 0.5 collective-permute-start.7
  41.2 1.6 %collective-permute-start.8 = (bf16[256,128]{1,0:T(8,128)(2,1)S(1)}, bf16[256,128]{1,0:T(8,128)(2,1)S(1)}, u32[]{:S(2)}, u32[]{:S(2)}) collective-permute-start(bf16[256,128]{1,0:T(8,128)(2,1)S(1)} %get-tuple-element.25), channel_id=1, source_target_pairs={{0,2},{1,3},{2,0},{3,1},{4,6},{5,7},{6,4},{7,5},{8,10},{9,11},{10,... | collective-permute-start | bytes 196616 | tf_op jit(solution)/shard_map/ppermute | solution.py:234
  42.8 0.0 collective-permute-start.9
  42.8 1.7 %collective-permute-start.10 = (bf16[256,128]{1,0:T(8,128)(2,1)S(1)}, bf16[256,128]{1,0:T(8,128)(2,1)S(1)}, u32[]{:S(2)}, u32[]{:S(2)}) collective-permute-start(bf16[256,128]{1,0:T(8,128)(2,1)S(1)} %get-tuple-element.27), channel_id=1, source_target_pairs={{0,4},{1,5},{2,6},{3,7},{4,0},{5,1},{6,2},{7,3},{8,12},{9,13},{10,... | collective-permute-start | bytes 196616 | tf_op jit(solution)/shard_map/ppermute | solution.py:234
  44.5 0.1 collective-permute-start.11
  44.7 0.0 collective-permute-done.7.refs_9_.refs_17_
  44.7 2.5 %collective-permute-start.12 = (bf16[256,128]{1,0:T(8,128)(2,1)S(1)}, bf16[256,128]{1,0:T(8,128)(2,1)S(1)}, u32[]{:S(2)}, u32[]{:S(2)}) collective-permute-start(bf16[256,128]{1,0:T(8,128)(2,1)S(1)} %get-tuple-element.29), channel_id=1, source_target_pairs={{0,6},{1,7},{2,4},{3,5},{4,2},{5,3},{6,0},{7,1},{8,14},{9,15},{10,... | collective-permute-start | bytes 196616 | tf_op jit(solution)/shard_map/ppermute | solution.py:234
  47.2 4.2 %collective-permute-done.8.refs_10_.refs_18_ = bf16[256,128]{1,0:T(8,128)(2,1)S(1)} collective-permute-done((bf16[256,128]{1,0:T(8,128)(2,1)S(1)}, bf16[256,128]{1,0:T(8,128)(2,1)S(1)}, u32[]{:S(2)}, u32[]{:S(2)}) %collective-permute-start.8) | collective-permute-done | bytes 65568 | tf_op jit(solution)/shard_map/ppermute | solution.py:234
  51.4 0.3 collective-permute-start.13
  51.8 0.0 collective-permute-done.9.refs_11_.refs_19_
  51.8 0.0 collective-permute-done.10.refs_12_.refs_20_
  51.8 0.0 collective-permute-done.11.refs_13_.refs_21_
  51.8 2.9 %collective-permute-done.12.refs_14_.refs_22_ = bf16[256,128]{1,0:T(8,128)(2,1)S(1)} collective-permute-done((bf16[256,128]{1,0:T(8,128)(2,1)S(1)}, bf16[256,128]{1,0:T(8,128)(2,1)S(1)}, u32[]{:S(2)}, u32[]{:S(2)}) %collective-permute-start.12) | collective-permute-done | bytes 65568 | tf_op jit(solution)/shard_map/ppermute | solution.py:234
  54.6 1.4 %collective-permute-done.13.refs_15_.refs_23_ = bf16[256,128]{1,0:T(8,128)(2,1)S(1)} collective-permute-done((bf16[256,128]{1,0:T(8,128)(2,1)S(1)}, bf16[256,128]{1,0:T(8,128)(2,1)S(1)}, u32[]{:S(2)}, u32[]{:S(2)}) %collective-permute-start.13) | collective-permute-done | bytes 65568 | tf_op jit(solution)/shard_map/ppermute | solution.py:234
  56.0 0.0 copy-done.1
  56.0 0.0 copy-done.2
  56.0 29.6 %shard_map.66.refs_10_ = bf16[512,4096]{1,0:T(8,128)(2,1)} custom-call(s32[1]{0:T(128)} %bitcast.place_ref.refs_0_, s32[2]{0:T(128)S(1)} %copy-done, s32[2]{0:T(128)S(1)} %copy-done.1, s32[16]{0:T(128)S(1)} %copy-done.2, bf16[512,4096]{1,0:T(8,128)(2,1)} %refs_4_.3, bf16[512,2,512]{2,1,0:T(2,128)(2,1)} %refs_5_.3, ...), custom_call_target="tpu_custom_call" | custom-call | flops 1073741824 | bytes 8388608 | tf_op jit(solution)/shard_map/pallas_call | solution.py:322
  85.6 0.0 all-to-all-done.1.refs_8_.refs_9_
  85.6 29.6 %shard_map.67 = bf16[512,4096]{1,0:T(8,128)(2,1)} custom-call(s32[1]{0:T(128)} %bitcast.place_ref.refs_0_, s32[2]{0:T(128)S(1)} %copy-done, s32[2]{0:T(128)S(1)} %copy-done.1, s32[16]{0:T(128)S(1)} %copy-done.2, bf16[512,4096]{1,0:T(8,128)(2,1)} %refs_4_.3, bf16[512,2,512]{2,1,0:T(2,128)(2,1)} %refs_5_.3, ...), custom_call_target="tpu_custom_call", output_to_operand_aliasing={{}: (10, {})} | custom-call | flops 1073741824 | bytes 8388608 | tf_op jit(solution)/shard_map/pallas_call | solution.py:322
Async XLA Ops:
  0.0 10.0 %copy-start = (s32[2]{0:T(128)S(1)}, s32[2]{0:T(128)}, u32[]{:S(2)}) copy-start(s32[2]{0:T(128)} %refs_1_.3) | copy-start | bytes 28
  2.6 30.3 %all-to-all-start = ((bf16[16,256,128]{2,1,0:T(8,128)(2,1)}), bf16[16,256,128]{2,1,0:T(8,128)(2,1)S(1)}, u32[]{:S(2)}, u32[]{:S(2)}) async-start(bf16[16,256,128]{2,1,0:T(8,128)(2,1)} %pad_maximum_fusion), calls=%async_computation | async-start | bytes 2097152 | tf_op jit(solution)/shard_map/all_to_all | solution.py:211
  10.0 18.4 %collective-permute-start.6 = (s32[2]{0:T(128)S(1)}, s32[2]{0:T(128)S(1)}, u32[]{:S(2)}, u32[]{:S(2)}) collective-permute-start(s32[2]{0:T(128)S(1)} %copy-done), channel_id=1, source_target_pairs={{0,7},{1,6},{2,5},{3,4},{4,3},{5,2},{6,1},{7,0},{8,15},{9,14},{10,... | collective-permute-start | bytes 32 | tf_op jit(solution)/shard_map/ppermute | solution.py:214
  12.6 17.1 %collective-permute-start.5 = (s32[2]{0:T(128)S(1)}, s32[2]{0:T(128)S(1)}, u32[]{:S(2)}, u32[]{:S(2)}) collective-permute-start(s32[2]{0:T(128)S(1)} %copy-done), channel_id=1, source_target_pairs={{0,6},{1,7},{2,4},{3,5},{4,2},{5,3},{6,0},{7,1},{8,14},{9,15},{10,... | collective-permute-start | bytes 32 | tf_op jit(solution)/shard_map/ppermute | solution.py:214
  13.0 16.7 %collective-permute-start.4 = (s32[2]{0:T(128)S(1)}, s32[2]{0:T(128)S(1)}, u32[]{:S(2)}, u32[]{:S(2)}) collective-permute-start(s32[2]{0:T(128)S(1)} %copy-done), channel_id=1, source_target_pairs={{0,5},{1,4},{2,7},{3,6},{4,1},{5,0},{6,3},{7,2},{8,13},{9,12},{10,... | collective-permute-start | bytes 32 | tf_op jit(solution)/shard_map/ppermute | solution.py:214
  14.3 15.4 %collective-permute-start.3 = (s32[2]{0:T(128)S(1)}, s32[2]{0:T(128)S(1)}, u32[]{:S(2)}, u32[]{:S(2)}) collective-permute-start(s32[2]{0:T(128)S(1)} %copy-done), channel_id=1, source_target_pairs={{0,4},{1,5},{2,6},{3,7},{4,0},{5,1},{6,2},{7,3},{8,12},{9,13},{10,... | collective-permute-start | bytes 32 | tf_op jit(solution)/shard_map/ppermute | solution.py:214
  14.6 15.1 %collective-permute-start.2 = (s32[2]{0:T(128)S(1)}, s32[2]{0:T(128)S(1)}, u32[]{:S(2)}, u32[]{:S(2)}) collective-permute-start(s32[2]{0:T(128)S(1)} %copy-done), channel_id=1, source_target_pairs={{0,3},{1,2},{2,1},{3,0},{4,7},{5,6},{6,5},{7,4},{8,11},{9,10},{10,... | collective-permute-start | bytes 32 | tf_op jit(solution)/shard_map/ppermute | solution.py:214
  22.2 33.8 %copy-start.1 = (s32[2]{0:T(128)S(1)}, s32[2]{0:T(128)}, u32[]{:S(2)}) copy-start(s32[2]{0:T(128)} %refs_2_.3) | copy-start | bytes 28
  22.2 33.8 %copy-start.2 = (s32[16]{0:T(128)S(1)}, s32[16]{0:T(128)}, u32[]{:S(2)}) copy-start(s32[16]{0:T(128)} %refs_3_.3) | copy-start | bytes 196
  28.3 3.6 %collective-permute-start.1 = (s32[2]{0:T(128)S(1)}, s32[2]{0:T(128)S(1)}, u32[]{:S(2)}, u32[]{:S(2)}) collective-permute-start(s32[2]{0:T(128)S(1)} %copy-done), channel_id=1, source_target_pairs={{0,2},{1,3},{2,0},{3,1},{4,6},{5,7},{6,4},{7,5},{8,10},{9,11},{10,... | collective-permute-start | bytes 32 | tf_op jit(solution)/shard_map/ppermute | solution.py:214
  29.7 2.3 %collective-permute-start = (s32[2]{0:T(128)S(1)}, s32[2]{0:T(128)S(1)}, u32[]{:S(2)}, u32[]{:S(2)}) collective-permute-start(s32[2]{0:T(128)S(1)} %copy-done), channel_id=1, source_target_pairs={{0,1},{1,0},{2,3},{3,2},{4,5},{5,4},{6,7},{7,6},{8,9},{9,8},{10,11... | collective-permute-start | bytes 32 | tf_op jit(solution)/shard_map/ppermute | solution.py:214
  34.9 50.8 %all-to-all-start.1 = ((bf16[8,256,128]{2,1,0:T(8,128)(2,1)}), bf16[8,256,128]{2,1,0:T(8,128)(2,1)S(1)}, u32[]{:S(2)}, u32[]{:S(2)}) async-start(bf16[8,256,128]{2,1,0:T(8,128)(2,1)} %get-tuple-element.22), calls=%async_computation.1 | async-start | bytes 1048576 | tf_op jit(solution)/shard_map/all_to_all | solution.py:235
  40.7 4.0 %collective-permute-start.7 = (bf16[256,128]{1,0:T(8,128)(2,1)S(1)}, bf16[256,128]{1,0:T(8,128)(2,1)S(1)}, u32[]{:S(2)}, u32[]{:S(2)}) collective-permute-start(bf16[256,128]{1,0:T(8,128)(2,1)S(1)} %get-tuple-element.24), channel_id=1, source_target_pairs={{0,1},{1,0},{2,3},{3,2},{4,5},{5,4},{6,7},{7,6},{8,9},{9,8},{10,11... | collective-permute-start | bytes 196616 | tf_op jit(solution)/shard_map/ppermute | solution.py:234
  41.2 10.3 %collective-permute-start.8 = (bf16[256,128]{1,0:T(8,128)(2,1)S(1)}, bf16[256,128]{1,0:T(8,128)(2,1)S(1)}, u32[]{:S(2)}, u32[]{:S(2)}) collective-permute-start(bf16[256,128]{1,0:T(8,128)(2,1)S(1)} %get-tuple-element.25), channel_id=1, source_target_pairs={{0,2},{1,3},{2,0},{3,1},{4,6},{5,7},{6,4},{7,5},{8,10},{9,11},{10,... | collective-permute-start | bytes 196616 | tf_op jit(solution)/shard_map/ppermute | solution.py:234
  42.8 9.0 %collective-permute-start.9 = (bf16[256,128]{1,0:T(8,128)(2,1)S(1)}, bf16[256,128]{1,0:T(8,128)(2,1)S(1)}, u32[]{:S(2)}, u32[]{:S(2)}) collective-permute-start(bf16[256,128]{1,0:T(8,128)(2,1)S(1)} %get-tuple-element.26), channel_id=1, source_target_pairs={{0,3},{1,2},{2,1},{3,0},{4,7},{5,6},{6,5},{7,4},{8,11},{9,10},{10,... | collective-permute-start | bytes 196616 | tf_op jit(solution)/shard_map/ppermute | solution.py:234
  42.8 9.0 %collective-permute-start.10 = (bf16[256,128]{1,0:T(8,128)(2,1)S(1)}, bf16[256,128]{1,0:T(8,128)(2,1)S(1)}, u32[]{:S(2)}, u32[]{:S(2)}) collective-permute-start(bf16[256,128]{1,0:T(8,128)(2,1)S(1)} %get-tuple-element.27), channel_id=1, source_target_pairs={{0,4},{1,5},{2,6},{3,7},{4,0},{5,1},{6,2},{7,3},{8,12},{9,13},{10,... | collective-permute-start | bytes 196616 | tf_op jit(solution)/shard_map/ppermute | solution.py:234
  44.5 7.2 %collective-permute-start.11 = (bf16[256,128]{1,0:T(8,128)(2,1)S(1)}, bf16[256,128]{1,0:T(8,128)(2,1)S(1)}, u32[]{:S(2)}, u32[]{:S(2)}) collective-permute-start(bf16[256,128]{1,0:T(8,128)(2,1)S(1)} %get-tuple-element.28), channel_id=1, source_target_pairs={{0,5},{1,4},{2,7},{3,6},{4,1},{5,0},{6,3},{7,2},{8,13},{9,12},{10,... | collective-permute-start | bytes 196616 | tf_op jit(solution)/shard_map/ppermute | solution.py:234
  44.7 10.0 %collective-permute-start.12 = (bf16[256,128]{1,0:T(8,128)(2,1)S(1)}, bf16[256,128]{1,0:T(8,128)(2,1)S(1)}, u32[]{:S(2)}, u32[]{:S(2)}) collective-permute-start(bf16[256,128]{1,0:T(8,128)(2,1)S(1)} %get-tuple-element.29), channel_id=1, source_target_pairs={{0,6},{1,7},{2,4},{3,5},{4,2},{5,3},{6,0},{7,1},{8,14},{9,15},{10,... | collective-permute-start | bytes 196616 | tf_op jit(solution)/shard_map/ppermute | solution.py:234
  51.4 4.6 %collective-permute-start.13 = (bf16[256,128]{1,0:T(8,128)(2,1)S(1)}, bf16[256,128]{1,0:T(8,128)(2,1)S(1)}, u32[]{:S(2)}, u32[]{:S(2)}) collective-permute-start(bf16[256,128]{1,0:T(8,128)(2,1)S(1)} %get-tuple-element.30), channel_id=1, source_target_pairs={{0,7},{1,6},{2,5},{3,4},{4,3},{5,2},{6,1},{7,0},{8,15},{9,14},{10,... | collective-permute-start | bytes 196616 | tf_op jit(solution)/shard_map/ppermute | solution.py:234
